TPU v7x, 256 devices: a whole 4x4x8 slice. The times are simulated.
256 devices in a mesh: dp: 8 (over z_lo, x), seq: 32 (over y, z_hi, core).
Axes of the slice: x: 4, y: 4, z: 8 (z_hi: 4, z_lo: 2; z = z_hi * 2 + z_lo), core: 2. Of those that a mesh axis runs over, the one named last changes fastest.
Arguments:
- queries: bfloat16 [8, 4096, 4096], P('dp', 'seq'), may hold values from -5 to 5
- rotated_key_rows: bfloat16 [8, 4096, 512], P('dp', 'seq'), may hold values from -5 to 5
- hidden_states: bfloat16 [8, 4096, 8192], P('dp', 'seq'), may hold values from -6 to 6
- block_order: int32 [64], replicated, may hold values from 0 to 63, each once
- first_weight: bfloat16 [8192, 512], replicated, may hold values from -0.0625 to 0.0625
- first_bias: float32 [512], replicated, may hold values from -3 to 3
- output_weight: bfloat16 [4, 512], replicated, may hold values from -0.25 to 0.25
- output_bias: float32 [4], replicated, may hold values from -1 to 1
Outputs:
- token_attention_mass: float32 [8, 4, 4096], P('dp', None, 'seq')
- loss_value: float32 [], replicated
- step_first: float32 [8192, 512], P('seq')
- output_weight_step: float32 [4, 512], replicated
- step_bias: float32 [512], replicated
- grad_bias: float32 [4], replicated
All inputs are finite; a program needn't handle non-finite values.
Results may differ from a plain program's by a relative error of at most 0.0023.
Values may be sent and summed in bfloat16 or wider, within the bound.
A program may use at most 64 MiB of HBM per device.

v0:
```python
import math
import jax
import jax.numpy as jnp
from jax import lax
from jax.sharding import PartitionSpec as P

D = 8192
KEY_VALUE_HEADS = 4
HEAD_SIZE = 128
RETAIN_HIDDEN = 512
BLK = 64
QUERY_GROUP_SIZE = 8


def key_places(block_order, offset, amount):
    row_ids = offset + lax.iota(jnp.int32, amount)
    block_ids = row_ids // BLK
    block_table = lax.iota(jnp.int32, block_order.shape[0])
    anchor = jnp.sum(
        jnp.where(block_ids[:, None] == block_table[None, :], block_order[None, :], 0), axis=1
    )
    return anchor * BLK + row_ids % BLK


def raw_scores(head_queries, mass_portion):
    head_keys = mass_portion.reshape(mass_portion.shape[0], KEY_VALUE_HEADS, HEAD_SIZE)
    return jnp.einsum(
        "tkgd,nkd->kgtn", head_queries, head_keys, preferred_element_type=jnp.float32
    ) * HEAD_SIZE ** (-0.5)


def blockwise(mass_portion, offset, update, carried):
    rows_here = mass_portion.shape[0]
    inner = math.gcd(rows_here, BLK)

    def visit_block(step_index, running):
        local_start = step_index * inner
        sub_rows = lax.dynamic_slice_in_dim(mass_portion, local_start, inner, 0)
        return update(running, sub_rows, offset + local_start)

    return lax.fori_loop(0, rows_here // inner, visit_block, carried)


def normalizer_step(running, mass_portion, key_start, head_queries, query_pos, block_order):
    highest, summed = running
    key_pos = key_places(block_order, key_start, mass_portion.shape[0])

    def normalizer_compute_step():
        scores = raw_scores(head_queries, mass_portion)
        visible = query_pos[:, None] >= key_pos[None, :]
        masked = jnp.where(visible, scores, -1e30)
        raised = jnp.maximum(highest, jnp.max(masked, axis=-1))
        exponents = jnp.where(visible, jnp.exp(masked - raised[..., None]), 0.0)
        return (raised, summed * jnp.exp(highest - raised) + jnp.sum(exponents, axis=-1))

    return lax.cond(
        jnp.min(key_pos) > jnp.max(query_pos), lambda: (highest, summed), normalizer_compute_step
    )


def mass_step(mass_portion, key_start, head_queries, query_pos, log_total, block_order):
    amount = mass_portion.shape[0]
    key_pos = key_places(block_order, key_start, amount)

    def mass_compute_step():
        scores = raw_scores(head_queries, mass_portion)
        visible = query_pos[:, None] >= key_pos[None, :]
        masked = jnp.where(visible, scores, -1e30)
        weights = jnp.where(visible, jnp.exp(masked - log_total[..., None]), 0.0)
        return jnp.sum(weights, axis=(1, 2)) / QUERY_GROUP_SIZE

    return lax.cond(
        jnp.min(key_pos) > jnp.max(query_pos),
        lambda: jnp.zeros((KEY_VALUE_HEADS, amount), jnp.float32),
        mass_compute_step,
    )


def normalized_scores(value_rows, square_sum, entries):
    return value_rows / jnp.sqrt(square_sum / entries + 1e-06)


def per_device(
    queries,
    rotated_key_rows,
    hidden_states,
    block_order,
    first_weight,
    first_bias,
    output_weight,
    output_bias,
):
    local_row_slice = queries.shape[1]
    total_length = local_row_slice * lax.axis_size("seq")
    head_queries = queries.reshape(local_row_slice, KEY_VALUE_HEADS, QUERY_GROUP_SIZE, HEAD_SIZE)
    local_key_rows = rotated_key_rows.reshape(local_row_slice, KEY_VALUE_HEADS * HEAD_SIZE)
    query_pos = key_places(block_order, lax.axis_index("seq") * local_row_slice, local_row_slice)
    start_state = (
        jnp.full((KEY_VALUE_HEADS, QUERY_GROUP_SIZE, local_row_slice), -1e30, jnp.float32),
        jnp.zeros((KEY_VALUE_HEADS, QUERY_GROUP_SIZE, local_row_slice), jnp.float32),
    )

    def norm_update(running, sub_rows, key_start):
        return normalizer_step(running, sub_rows, key_start, head_queries, query_pos, block_order)

    empty_mass = jnp.zeros((KEY_VALUE_HEADS, total_length), jnp.float32)
    keys_whole = lax.all_gather(local_key_rows, "seq", axis=0, tiled=True)
    highest, summed = blockwise(keys_whole, 0, norm_update, start_state)
    log_total = highest + jnp.log(summed)

    def add_kept(collected, sub_rows, key_start):
        term = mass_step(sub_rows, key_start, head_queries, query_pos, log_total, block_order)
        return lax.dynamic_update_slice_in_dim(collected, term, key_start, 1)

    column_mass = blockwise(keys_whole, 0, add_kept, empty_mass)
    key_attention_mass = lax.psum_scatter(column_mass, "seq", scatter_dimension=1, tiled=True)
    tokens_in = hidden_states.reshape(local_row_slice, hidden_states.shape[2])
    pre_act = jnp.dot(tokens_in, first_weight, preferred_element_type=jnp.float32) + first_bias
    hidden = jax.nn.silu(pre_act).astype(jnp.bfloat16)
    predicted_scores = (
        lax.dot_general(
            output_weight, hidden, (((1,), (1,)), ((), ())), preferred_element_type=jnp.float32
        )
        + output_bias[:, None]
    )
    score_residue = predicted_scores - jnp.log(1.0 + key_attention_mass)
    loss_part = 0.5 * jnp.sum(score_residue * score_residue) / total_length
    out_grad = score_residue / total_length
    bias_part = jnp.sum(out_grad, axis=1)
    second_part = jnp.dot(out_grad, hidden.astype(jnp.float32), precision=lax.Precision.HIGHEST)
    back_grad = jnp.dot(
        out_grad.T, output_weight.astype(jnp.float32), precision=lax.Precision.HIGHEST
    )
    gate_value = jax.nn.sigmoid(pre_act)
    slope_grad = back_grad * gate_value * (1.0 + pre_act * (1.0 - gate_value))
    first_bias_part = jnp.sum(slope_grad, axis=0)
    slope_half = slope_grad.astype(jnp.bfloat16)
    columns_all = lax.all_to_all(tokens_in, "seq", split_axis=1, concat_axis=0, tiled=True)
    slope_all = lax.all_gather(slope_half, "seq", axis=0, tiled=True)
    first_shard = lax.dot_general(
        columns_all, slope_all, (((0,), (0,)), ((), ())), preferred_element_type=jnp.float32
    )
    output_total, first_bias_total, bias_total, loss_total = lax.psum(
        (second_part, first_bias_part, bias_part, loss_part), ("dp", "seq")
    )
    first_grad = lax.psum(first_shard, "dp")
    first_square = lax.psum(jnp.sum(first_grad * first_grad), "seq")
    step_first = normalized_scores(first_grad, first_square, D * RETAIN_HIDDEN)
    output_weight_step = normalized_scores(
        output_total, jnp.sum(output_total * output_total), RETAIN_HIDDEN * KEY_VALUE_HEADS
    )
    step_bias = normalized_scores(
        first_bias_total, jnp.sum(first_bias_total * first_bias_total), RETAIN_HIDDEN
    )
    return (
        key_attention_mass.reshape(1, KEY_VALUE_HEADS, local_row_slice),
        loss_total,
        step_first,
        output_weight_step,
        step_bias,
        bias_total,
    )


def solution(mesh):
    in_specs = (
        P("dp", "seq", None),
        P("dp", "seq", None),
        P("dp", "seq", None),
        P(),
        P(),
        P(),
        P(),
        P(),
    )
    out_specs = (P("dp", None, "seq"), P(), P("seq", None), P(), P(), P())
    return jax.shard_map(
        per_device, mesh=mesh, in_specs=in_specs, out_specs=out_specs, check_vma=False
    )
```

profile of v0, /device:TPU:1, one launch (start us, length us, event | category | flops | bytes accessed | tf_op | source)
XLA Modules:
  0.0 925.9 jit_solution(2229353486682803280)
XLA Ops:
  11.0 64.1 %all-gather.6.cloned.1.call-done = bf16[1,4096,512]{2,1,0:T(8,128)(2,1)} async-done(((bf16[1,128,512]{2,1,0:T(8,128)(2,1)}), bf16[1,4096,512]{2,1,0:T(8,128)(2,1)}) %all-gather.6.cloned.1.call-update) | async-done | bytes 4194320 | tf_op jit(solution)/shard_map/all_gather | solution.py:107
  75.1 206.3 %while.32 = (s32[]{:T(128)}, f32[4,8,128]{2,1,0:T(8,128)S(1)}, f32[4,8,128]{2,1,0:T(8,128)S(1)}, s32[64]{0:T(128)S(1)}, s32[]{:T(128)}, /*index=5*/s32[128]{0:T(...) while((s32[]{:T(128)}, f32[4,8,128]{2,1,0:T(8,128)S(1)}, ...), condition=%wide.region_9.10_spmd, body=%wide.region_2.9_spmd.sunk | while | flops 68712320 | bytes 3713545 | solution.py:41
  79.5 1.7 conditional.4
  83.4 1.7 conditional.4
  87.3 1.7 conditional.4
  91.3 1.7 conditional.4
  108.4 1.7 conditional.4
  112.3 1.7 conditional.4
  118.5 1.7 conditional.4
  122.4 1.7 conditional.4
  128.5 1.7 conditional.4
  132.4 1.7 conditional.4
  138.6 1.7 conditional.4
  144.7 1.7 conditional.4
  153.0 1.7 conditional.4
  156.9 1.7 conditional.4
  160.9 1.7 conditional.4
  169.2 1.7 conditional.4
  173.1 1.7 conditional.4
  181.0 1.7 conditional.4
  184.9 1.7 conditional.4
  193.2 1.7 conditional.4
  199.3 1.7 conditional.4
  213.8 1.7 conditional.4
  217.7 1.7 conditional.4
  221.6 1.7 conditional.4
  225.6 1.7 conditional.4
  231.7 1.7 conditional.4
  235.6 1.7 conditional.4
  239.5 1.7 conditional.4
  249.6 1.7 conditional.4
  253.5 1.7 conditional.4
  257.4 1.7 conditional.4
  265.2 1.7 conditional.4
  269.1 1.7 conditional.4
  279.7 1.7 conditional.4
  281.5 212.6 %while.33 = (s32[]{:T(128)}, f32[4,4096]{1,0:T(4,128)S(1)}, s32[64]{0:T(128)S(1)}, s32[]{:T(128)}, s32[128]{0:T(128)S(1)}, /*index=5*/bf16[4096,512]{1,0:T(8,128...) while((s32[]{:T(128)}, f32[4,4096]{1,0:T(4,128)S(1)}, ...), condition=%wide.region_16.17_spmd, body=%wide.region_10.16_spmd.sunk | while | flops 68441992 | bytes 1416701 | solution.py:41
  494.1 2.0 copy.51
  496.2 4.8 multiply_convert_fusion
  501.0 164.5 %reduce-scatter.4.cloned.1.call-done = f32[128,4]{1,0:T(8,128)} async-done(((f32[4096,4]{1,0:T(8,128)}), f32[128,4]{1,0:T(8,128)}) %reduce-scatter.4.cloned.1.call-update) | async-done | bytes 2064
  668.3 2.5 copy.42
  670.8 63.7 %all_to_all.19 = bf16[128,32,256]{0,2,1:T(8,128)(2,1)S(1)} all-to-all(bf16[128,32,256]{0,2,1:T(8,128)(2,1)} %bitcast.50), channel_id=1, replica_groups=mesh['dp'=8,'seq'=32] {'seq'}, dimensions={1} | all-to-all | bytes 4194304 | tf_op jit(solution)/shard_map/all_to_all | solution.py:138
  734.5 2.9 copy.43
  737.4 19.9 %all-gather.4.cloned.1.call-done = bf16[4096,512]{1,0:T(8,128)(2,1)} async-done(((bf16[128,512]{1,0:T(8,128)(2,1)}), bf16[4096,512]{1,0:T(8,128)(2,1)}) %all-gather.4.cloned.1.call-update) | async-done | bytes 4194320 | tf_op jit(solution)/shard_map/all_gather | solution.py:139
  757.3 4.9 convolution_bitcast_fusion
  763.1 77.0 %all-reduce = (f32[]{:T(128)}, f32[4,512]{1,0:T(4,128)S(1)}, f32[512]{0:T(512)S(1)}, f32[4]{0:T(128)}) all-reduce(f32[]{:T(128)S(6)} %div.87, f32[4,512]{1,0:T(4,128)S(1)} %fusion.20, f32[512]{0:T(512)S(1)} %get-tuple-element.630, f32[4]{0:T(128)S(1)} %get-tuple-element.583), channel_id=1, replica_groups=mesh['dp'=8,'seq'=32] {'dp','seq'}, use_global_device_ids=true, to_apply=%region_19.20 | all-reduce | flops 2565 | bytes 20520 | tf_op jit(solution)/shard_map/psum | solution.py:143
  843.3 1.8 multiply_reduce_fusion
  845.7 70.9 %psum.44 = f32[]{:T(128)} all-reduce(f32[]{:T(128)} %multiply_reduce_fusion), channel_id=1, replica_groups=mesh['dp'=8,'seq'=32] {'seq'}, use_global_device_ids=true, to_apply=%region_22.23 | all-reduce | flops 1 | bytes 8 | tf_op jit(solution)/shard_map/psum | solution.py:147
  (1154 shorter events, 322.9 us)
Async XLA Ops:
  7.2 659.3 %copy-start = (bf16[4,512]{1,0:T(4,128)(2,1)S(1)}, bf16[4,512]{1,0:T(4,128)(2,1)}, u32[]{:S(2)}) copy-start(bf16[4,512]{1,0:T(4,128)(2,1)} %param.22) | copy-start | bytes 12292
  7.2 3.1 copy-start.4
  7.2 67.9 %all-gather.6.cloned.1.call-start = ((), (), s32[]{:S(2)}) async-start(), calls=%async_computation.4 | async-start | bytes 4325376 | tf_op jit(solution)/shard_map/all_gather | solution.py:107
  7.9 657.6 %reduce-scatter.4.cloned.1.call-start = ((), (), s32[]{:S(2)}) async-start(), calls=%async_computation.5 | async-start | bytes 2162688
  494.1 2.1 copy-start.1
  494.1 2.1 copy-start.2
  496.1 170.4 %copy-start.5 = (f32[4]{0:T(128)S(1)}, f32[4]{0:T(128)}, u32[]{:S(2)}) copy-start(f32[4]{0:T(128)} %param.23) | copy-start | bytes 52
  496.1 261.2 %all-gather.4.cloned.1.call-start = ((), (), s32[]{:S(2)}) async-start(), calls=%async_computation.2 | async-start | bytes 4325376 | tf_op jit(solution)/shard_map/all_gather | solution.py:139
  666.4 68.1 %copy-start.3 = (f32[4,128]{1,0:T(4,128)}, f32[4,128]{1,0:T(4,128)S(1)}, u32[]{:S(2)}) copy-start(f32[4,128]{1,0:T(4,128)S(1)} %copy.52) | copy-start | bytes 6148
  668.2 175.1 %all-reduce.3.cloned.1.call-start = ((), (), s32[]{:S(2)}) async-start(), calls=%async_computation.3 | async-start | bytes 1048576 | tf_op jit(solution)/shard_map/psum | solution.py:146
Sparse Core Ops, SparseCore 0:
  10.6 64.5 all-gather.5
  496.2 169.2 reduce-scatter.3
  668.7 88.6 all-gather.3
  762.4 72.5 all-reduce.2
where the time goes:
time: 935 us; the launch traced here: 926 us
  waiting for transfers between devices  249 us (27%)
  blocking collectives  212 us (23%)
  loops' own time  175 us (19%)
  other arithmetic  128 us (14%)
  local copies, waits for them, and re-layouts  92.1 us (10%)
  matrix products  52.9 us (6%)
  between operations  16.7 us (2%)
    another operation x2, loops' own time, blockwise(): return lax.fori_loop(0, rows_here // inner, visit_block, carried)  171 us
    unnamed x5, waiting for transfers between devices  165 us
    psum x1, blocking collectives, per_device(): lax.psum((second_part, first_bias_part, bias_part, loss_part), ('dp', 'se...  77 us
    psum x1, blocking collectives, per_device(): first_square = lax.psum(jnp.sum(first_grad * first_grad), 'seq')  70.9 us
    dynamic_slice x76, local copies, waits for them, and re-layouts, visit_block(): sub_rows = lax.dynamic_slice_in_dim(mass_portion, local_start, inner, 0)  64.7 us
    all_gather x1, waiting for transfers between devices, per_device(): keys_whole = lax.all_gather(local_key_rows, 'seq', axis=0, tiled=True)  64.1 us
    all_to_all x1, blocking collectives, per_device(): lax.all_to_all(tokens_in, 'seq', split_axis=1, concat_axis=0, tiled=True)  63.7 us
    reduce_min x64, other arithmetic, normalizer_step(): jnp.min(key_pos) > jnp.max(query_pos)  41.8 us
  transfers between devices with their start and end apart: 4, of which 3 were waited for; matrix products, arithmetic and copies ran while one was open for 2% of the time, Pallas kernels for 0%

commit v1 on v0

--- a/solution.py
+++ b/solution.py
@@ -104,7 +104,9 @@
         return normalizer_step(running, sub_rows, key_start, head_queries, query_pos, block_order)
 
     empty_mass = jnp.zeros((KEY_VALUE_HEADS, total_length), jnp.float32)
-    keys_whole = lax.all_gather(local_key_rows, "seq", axis=0, tiled=True)
+    keys_whole = jnp.concatenate(
+        lax.all_to_all(jnp.stack([local_key_rows] * lax.axis_size("seq")), "seq", 0, 0), axis=0
+    )
     highest, summed = blockwise(keys_whole, 0, norm_update, start_state)
     log_total = highest + jnp.log(summed)
 

time: 935 us -> 980 us (1.048)
  waiting for transfers between devices: 249 us -> 279 us
  starting transfers between devices: 0.16 us -> 13.1 us
    all_to_all x0 -> x1, waiting for transfers between devices: none -> 91.1 us  [per_device(): lax.all_to_all(jnp.stack([local_key_rows] * lax.axis_size('seq')), 'seq',...]
    all_gather x1 -> x0, waiting for transfers between devices: 64.1 us -> none  [per_device(): keys_whole = lax.all_gather(local_key_rows, 'seq', axis=0, tiled=True)]
    all_to_all x0 -> x1, starting transfers between devices: none -> 12.9 us  [per_device(): lax.all_to_all(jnp.stack([local_key_rows] * lax.axis_size('seq')), 'seq',...]
    unnamed x5 -> x4, waiting for transfers between devices: 165 us -> 167 us
  transfers between devices with their start and end apart: 4 -> 4, of which waited for: 3 -> 3; matrix products, arithmetic and copies ran while one was open for 2% -> 1% of each run, Pallas kernels for 0% -> 0%
where the time goes in v1:
time: 980 us; the launch traced here: 971 us
  waiting for transfers between devices  279 us (28%)
  blocking collectives  212 us (22%)
  loops' own time  175 us (18%)
  other arithmetic  128 us (13%)
  local copies, waits for them, and re-layouts  94.4 us (10%)
  matrix products  53.1 us (5%)
  between operations  16.6 us (2%)
  starting transfers between devices  13.1 us (1%)
    another operation x2, loops' own time, blockwise(): return lax.fori_loop(0, rows_here // inner, visit_block, carried)  171 us
    unnamed x4, waiting for transfers between devices  167 us
    all_to_all x1, waiting for transfers between devices, per_device(): lax.all_to_all(jnp.stack([local_key_rows] * lax.axis_size('seq')), 'seq',...  91.1 us
    psum x1, blocking collectives, per_device(): lax.psum((second_part, first_bias_part, bias_part, loss_part), ('dp', 'se...  77.2 us
    psum x1, blocking collectives, per_device(): first_square = lax.psum(jnp.sum(first_grad * first_grad), 'seq')  71 us
    dynamic_slice x76, local copies, waits for them, and re-layouts, visit_block(): sub_rows = lax.dynamic_slice_in_dim(mass_portion, local_start, inner, 0)  64.6 us
    all_to_all x1, blocking collectives, per_device(): lax.all_to_all(tokens_in, 'seq', split_axis=1, concat_axis=0, tiled=True)  63.8 us
    reduce_min x64, other arithmetic, mass_step(): jnp.min(key_pos) > jnp.max(query_pos)  41.8 us
  transfers between devices with their start and end apart: 4, of which 3 were waited for; matrix products, arithmetic and copies ran while one was open for 1% of the time, Pallas kernels for 0%

profile of v1, /device:TPU:1, one launch (start us, length us, event | category | flops | bytes accessed | tf_op | source)
XLA Modules:
  0.0 971.1 jit_solution(12285058296067650924)
XLA Ops:
  7.2 3.4 stack.3
  10.5 12.9 %all-to-all-start = ((bf16[32,128,512]{2,1,0:T(8,128)(2,1)}), bf16[32,128,512]{2,1,0:T(8,128)(2,1)}, u32[]{:S(2)}, u32[]{:S(2)}) async-start(bf16[32,128,512]{2,1,0:T(8,128)(2,1)} %stack.3), calls=%async_computation | async-start | bytes 8388608 | tf_op jit(solution)/shard_map/all_to_all | solution.py:108
  25.7 91.1 %all-to-all-done = bf16[32,128,512]{2,1,0:T(8,128)(2,1)} async-done(((bf16[32,128,512]{2,1,0:T(8,128)(2,1)}), bf16[32,128,512]{2,1,0:T(8,128)(2,1)}, u32[]{:S(2)}, u32[]{:S(2)}) %all-to-all-start) | async-done | bytes 4194336 | tf_op jit(solution)/shard_map/all_to_all | solution.py:108
  116.7 206.4 %while.32 = (s32[]{:T(128)}, f32[4,8,128]{2,1,0:T(8,128)S(1)}, f32[4,8,128]{2,1,0:T(8,128)S(1)}, s32[64]{0:T(128)S(1)}, s32[]{:T(128)}, /*index=5*/s32[128]{0:T(...) while((s32[]{:T(128)}, f32[4,8,128]{2,1,0:T(8,128)S(1)}, ...), condition=%wide.region_9.10_spmd, body=%wide.region_2.9_spmd.sunk | while | flops 68712320 | bytes 3713545 | solution.py:41
  121.1 1.7 conditional.4
  125.0 1.7 conditional.4
  128.9 1.7 conditional.4
  132.9 1.7 conditional.4
  150.1 1.7 conditional.4
  154.0 1.7 conditional.4
  160.1 1.7 conditional.4
  164.0 1.7 conditional.4
  174.1 1.7 conditional.4
  180.2 1.7 conditional.4
  186.3 1.7 conditional.4
  194.7 1.7 conditional.4
  198.6 1.7 conditional.4
  202.5 1.7 conditional.4
  210.8 1.7 conditional.4
  214.8 1.7 conditional.4
  218.7 1.7 conditional.4
  222.6 1.7 conditional.4
  226.5 1.7 conditional.4
  234.9 1.7 conditional.4
  244.9 1.7 conditional.4
  259.4 1.7 conditional.4
  263.3 1.7 conditional.4
  267.2 1.7 conditional.4
  277.3 1.7 conditional.4
  281.2 1.7 conditional.4
  285.1 1.7 conditional.4
  295.1 1.7 conditional.4
  299.0 1.7 conditional.4
  303.0 1.7 conditional.4
  306.9 1.7 conditional.4
  310.8 1.7 conditional.4
  323.2 212.7 %while.33 = (s32[]{:T(128)}, f32[4,4096]{1,0:T(4,128)S(1)}, s32[64]{0:T(128)S(1)}, s32[]{:T(128)}, s32[128]{0:T(128)S(1)}, /*index=5*/bf16[4096,512]{1,0:T(8,128...) while((s32[]{:T(128)}, f32[4,4096]{1,0:T(4,128)S(1)}, ...), condition=%wide.region_16.17_spmd, body=%wide.region_10.16_spmd.sunk | while | flops 68441992 | bytes 1416701 | solution.py:41
  535.9 2.0 copy.51
  538.0 4.8 multiply_convert_fusion
  542.8 166.6 %reduce-scatter.4.cloned.1.call-done = f32[128,4]{1,0:T(8,128)} async-done(((f32[4096,4]{1,0:T(8,128)}), f32[128,4]{1,0:T(8,128)}) %reduce-scatter.4.cloned.1.call-update) | async-done | bytes 2064
  712.1 2.5 copy.42
  714.6 63.8 %all_to_all.24 = bf16[128,32,256]{0,2,1:T(8,128)(2,1)S(1)} all-to-all(bf16[128,32,256]{0,2,1:T(8,128)(2,1)} %bitcast.51), channel_id=1, replica_groups=mesh['dp'=8,'seq'=32] {'seq'}, dimensions={1} | all-to-all | bytes 4194304 | tf_op jit(solution)/shard_map/all_to_all | solution.py:140
  778.4 2.9 copy.43
  781.3 21.0 %all-gather.2.cloned.1.call-done = bf16[4096,512]{1,0:T(8,128)(2,1)} async-done(((bf16[128,512]{1,0:T(8,128)(2,1)}), bf16[4096,512]{1,0:T(8,128)(2,1)}) %all-gather.2.cloned.1.call-update) | async-done | bytes 4194320 | tf_op jit(solution)/shard_map/all_gather | solution.py:141
  802.3 4.9 convolution_bitcast_fusion
  808.1 77.2 %all-reduce = (f32[]{:T(128)}, f32[4,512]{1,0:T(4,128)S(1)}, f32[512]{0:T(512)S(1)}, f32[4]{0:T(128)}) all-reduce(f32[]{:T(128)S(6)} %div.87, f32[4,512]{1,0:T(4,128)S(1)} %fusion.20, f32[512]{0:T(512)S(1)} %get-tuple-element.630, f32[4]{0:T(128)S(1)} %get-tuple-element.583), channel_id=1, replica_groups=mesh['dp'=8,'seq'=32] {'dp','seq'}, use_global_device_ids=true, to_apply=%region_19.20 | all-reduce | flops 2565 | bytes 20520 | tf_op jit(solution)/shard_map/psum | solution.py:145
  888.5 1.8 multiply_reduce_fusion
  890.8 71.0 %psum.44 = f32[]{:T(128)} all-reduce(f32[]{:T(128)} %multiply_reduce_fusion), channel_id=1, replica_groups=mesh['dp'=8,'seq'=32] {'seq'}, use_global_device_ids=true, to_apply=%region_22.23 | all-reduce | flops 1 | bytes 8 | tf_op jit(solution)/shard_map/psum | solution.py:149
  (1156 shorter events, 325.0 us)
Async XLA Ops:
  7.2 703.1 %copy-start = (bf16[4,512]{1,0:T(4,128)(2,1)S(1)}, bf16[4,512]{1,0:T(4,128)(2,1)}, u32[]{:S(2)}) copy-start(bf16[4,512]{1,0:T(4,128)(2,1)} %param.22) | copy-start | bytes 12292
  10.5 13.0 %copy-start.2 = (bf16[1,128,4096]{2,1,0:T(8,128)(2,1)S(1)}, bf16[1,128,4096]{2,1,0:T(8,128)(2,1)}, u32[]{:S(2)}) copy-start(bf16[1,128,4096]{2,1,0:T(8,128)(2,1)} %param.16) | copy-start | bytes 3145732
  10.5 106.2 %all-to-all-start = ((bf16[32,128,512]{2,1,0:T(8,128)(2,1)}), bf16[32,128,512]{2,1,0:T(8,128)(2,1)}, u32[]{:S(2)}, u32[]{:S(2)}) async-start(bf16[32,128,512]{2,1,0:T(8,128)(2,1)} %stack.3), calls=%async_computation | async-start | bytes 8388608 | tf_op jit(solution)/shard_map/all_to_all | solution.py:108
  23.5 1.4 copy-start.5
  23.5 685.9 %reduce-scatter.4.cloned.1.call-start = ((), (), s32[]{:S(2)}) async-start(), calls=%async_computation.5 | async-start | bytes 2162688
  535.9 2.1 copy-start.1
  535.9 2.1 copy-start.3
  537.9 172.4 %copy-start.6 = (f32[4]{0:T(128)S(1)}, f32[4]{0:T(128)}, u32[]{:S(2)}) copy-start(f32[4]{0:T(128)} %param.23) | copy-start | bytes 52
  537.9 264.4 %all-gather.2.cloned.1.call-start = ((), (), s32[]{:S(2)}) async-start(), calls=%async_computation.3 | async-start | bytes 4325376 | tf_op jit(solution)/shard_map/all_gather | solution.py:141
  710.3 68.1 %copy-start.4 = (f32[4,128]{1,0:T(4,128)}, f32[4,128]{1,0:T(4,128)S(1)}, u32[]{:S(2)}) copy-start(f32[4,128]{1,0:T(4,128)S(1)} %copy.52) | copy-start | bytes 6148
  712.1 176.4 %all-reduce.3.cloned.1.call-start = ((), (), s32[]{:S(2)}) async-start(), calls=%async_computation.4 | async-start | bytes 1048576 | tf_op jit(solution)/shard_map/psum | solution.py:148
Sparse Core Ops, SparseCore 0:
  538.0 171.3 reduce-scatter.3
  712.5 89.7 all-gather.1
  807.4 72.5 all-reduce.2
